TPU v7x, 128 devices: a whole 4x4x4 slice. The times are simulated.
128 devices in a mesh: grp: 2 (over z_lo), fsdp: 16 (over x, z_hi, core), item: 4 (over y).
Axes of the slice: x: 4, y: 4, z: 4 (z_hi: 2, z_lo: 2; z = z_hi * 2 + z_lo), core: 2. Of those that a mesh axis runs over, the one named last changes fastest.
Arguments:
- hidden_states: bfloat16 [8192, 16, 4096], P(('grp', 'fsdp', 'item')), may hold values from -6 to 6
- positives: bfloat16 [8192, 1024], P(('grp', 'fsdp', 'item')), may hold values from -6 to 6
- negatives: int32 [8192, 32], P(('grp', 'fsdp', 'item')), may hold values from 0 to 4095, as said below
- lengths: int32 [8192], P(('grp', 'fsdp', 'item')), may hold values from 1 to 16, as said below
- norm_gain: bfloat16 [4096], replicated, may hold values from 0.25 to 1.75
- proj_weight: bfloat16 [4096, 1024], P('fsdp'), may hold values from -0.09375 to 0.09375
- pool_query: float32 [1024], replicated, may hold values from -6 to 6
- slab: bfloat16 [4096, 1024], P('item'), may hold values from -6 to 6
Outputs:
- grad_proj: float32 [4096, 1024], P('fsdp')
- grad_query: float32 [1024], replicated
- mean_loss: float32 [], replicated
Inputs may be any that keep to these rules, and one draw needn't show every extreme that they name: `negatives`: entries 8 o to 8 (o + 1) - 1 of each query's list are rows of owner block o, the slab rows 1024 o to 1024 (o + 1) - 1; a row may repeat. The first lengths[q] token slots of query q are valid.
All inputs are finite; a program needn't handle non-finite values.
Results may differ from a plain program's by a relative error of at most 0.0043.
Values may be sent and summed in bfloat16 or wider, within the bound.
A program may use at most 128 MiB of HBM per device.

v0:
```python
import math

import jax
import jax.numpy as jnp
from jax import lax
from jax.sharding import PartitionSpec as P

sharpness_divisor = 0.05
norm_eps = 1e-05
embed_eps = 1e-06


def normalize(states, norm_gain):
    flat_states = states.reshape(-1, states.shape[-1]).astype(jnp.float32)
    inv_rms = lax.rsqrt(jnp.mean(flat_states * flat_states, axis=1, keepdims=True) + norm_eps)
    return (flat_states * inv_rms * norm_gain.astype(jnp.float32)).astype(jnp.bfloat16)


def gated_pool(token_proj, lengths, pool_query, seq_len):
    queries = lengths.shape[0]
    proj_width = token_proj.shape[1]
    tokens = token_proj.reshape(queries, seq_len, proj_width)
    gate_vals = jax.nn.sigmoid(
        jnp.einsum("qsp,p->qs", tokens, pool_query, precision=lax.Precision.HIGHEST)
        / math.sqrt(proj_width)
    )
    position = lax.broadcasted_iota(jnp.int32, (queries, seq_len), 1)
    weight = jnp.where(position < lengths[:, None], 1.0, 0.0).astype(jnp.float32) / lengths[
        :, None
    ].astype(jnp.float32)
    pooled = jnp.einsum("qs,qsp->qp", weight * gate_vals, tokens, precision=lax.Precision.HIGHEST)
    return (pooled, gate_vals, weight)


def unit_embed(pooled):
    proj_width = pooled.shape[1]
    unit_scale = lax.rsqrt(
        jnp.mean(pooled * pooled, axis=1, keepdims=True) + embed_eps
    ) / math.sqrt(proj_width)
    return ((pooled * unit_scale).astype(jnp.bfloat16), unit_scale)


def contrast(embedded, positives, neg_rows):
    proj_width = embedded.shape[1]
    matching_vector_fullprec = positives.astype(jnp.float32)
    matching_multiplier = lax.rsqrt(
        jnp.mean(matching_vector_fullprec * matching_vector_fullprec, axis=1) + embed_eps
    ) / math.sqrt(proj_width)
    matching_score = (
        jnp.einsum(
            "au,au->a",
            embedded.astype(jnp.float32),
            matching_vector_fullprec,
            precision=lax.Precision.HIGHEST,
        )
        * matching_multiplier
        / sharpness_divisor
    )
    row_sq = jnp.einsum("qnp,qnp->qn", neg_rows, neg_rows, preferred_element_type=jnp.float32)
    sample_multiplier = lax.rsqrt(row_sq / proj_width + embed_eps) / math.sqrt(proj_width)
    distractor_score = (
        jnp.einsum("ir,isr->is", embedded, neg_rows, preferred_element_type=jnp.float32)
        * sample_multiplier
        / sharpness_divisor
    )
    logits = jnp.concatenate([matching_score[:, None], distractor_score], axis=1)
    exp_logits = jnp.exp(logits)
    denom_sum = jnp.sum(exp_logits, axis=1, keepdims=True)
    prob = exp_logits / denom_sum
    loss_sum = jnp.sum(jnp.log(denom_sum[:, 0]) - matching_score)
    column = lax.broadcasted_iota(jnp.int32, logits.shape, 1)
    score_derivative = prob - jnp.where(column == 0, 1.0, 0.0).astype(jnp.float32)
    matching_contribution = (score_derivative[:, 0] * matching_multiplier / sharpness_divisor)[
        :, None
    ] * matching_vector_fullprec
    distractor_probability = (
        score_derivative[:, 1:] * sample_multiplier / sharpness_divisor
    ).astype(jnp.bfloat16)
    grad_embed = matching_contribution + jnp.einsum(
        "qn,qnp->qp", distractor_probability, neg_rows, preferred_element_type=jnp.float32
    )
    return (loss_sum, grad_embed)


def backward(token_proj, pooled, unit_scale, grad_embed, gate_vals, weight, pool_query, seq_len):
    queries, proj_width = pooled.shape
    tokens = token_proj.reshape(queries, seq_len, proj_width)
    mean_sq = jnp.mean(pooled * pooled, axis=1, keepdims=True)
    radial = jnp.sum(pooled * grad_embed, axis=1, keepdims=True)
    grad_pooled = unit_scale * grad_embed - pooled * radial * unit_scale / (
        proj_width * (mean_sq + embed_eps)
    )
    proj_dot = jnp.einsum("qsp,qp->qs", tokens, grad_pooled, precision=lax.Precision.HIGHEST)
    gate_slope = weight * gate_vals * (1.0 - gate_vals) * proj_dot / math.sqrt(proj_width)
    grad_tokens = (weight * gate_vals)[:, :, None] * grad_pooled[:, None, :] + gate_slope[
        :, :, None
    ] * pool_query[None, None, :]
    grad_query = jnp.einsum("qs,qsp->p", gate_slope, tokens, precision=lax.Precision.HIGHEST)
    return (grad_tokens.reshape(queries * seq_len, proj_width).astype(jnp.bfloat16), grad_query)


def body(hidden_states, positives, negatives, lengths, norm_gain, proj_weight, pool_query, slab):
    queries, seq_len, model_width = hidden_states.shape
    proj_width = proj_weight.shape[1]
    neg_count = negatives.shape[1]
    normed = normalize(hidden_states, norm_gain)

    def add_rows(shard_rows):
        return jnp.dot(normed, shard_rows, preferred_element_type=jnp.float32)

    def project():
        return add_rows(lax.all_gather(proj_weight, "fsdp", axis=0, tiled=True))

    token_proj = project()
    pooled, gate_vals, weight = gated_pool(token_proj, lengths, pool_query, seq_len)
    embedded, unit_scale = unit_embed(pooled)
    slab_piece = lax.all_gather(slab, "item", axis=0, tiled=True)
    inside = (negatives >= 0) & (negatives < slab_piece.shape[0])
    picked = jnp.take(slab_piece, jnp.clip(negatives, 0, slab_piece.shape[0] - 1), axis=0)
    neg_rows = jnp.where(
        inside[:, :, None], picked, jnp.zeros((queries, neg_count, proj_width), jnp.bfloat16)
    )
    loss_part, grad_embed = contrast(embedded, positives, neg_rows)
    token_proj = project()
    pooled, gate_vals, weight = gated_pool(token_proj, lengths, pool_query, seq_len)
    embedded, unit_scale = unit_embed(pooled)
    grad_tokens, query_part = backward(
        token_proj, pooled, unit_scale, grad_embed, gate_vals, weight, pool_query, seq_len
    )
    grad_shard = lax.psum_scatter(
        lax.dot_general(
            normed, grad_tokens, (((0,), (0,)), ((), ())), preferred_element_type=jnp.float32
        ),
        "fsdp",
        scatter_dimension=0,
        tiled=True,
    )
    grad_proj = lax.psum(grad_shard, ("grp", "item"))
    grad_query, loss_total = lax.psum((query_part, loss_part), ("grp", "fsdp", "item"))
    all_queries = queries * lax.axis_size("grp") * lax.axis_size("fsdp") * lax.axis_size("item")
    mean_loss = loss_total / all_queries
    return (grad_proj, grad_query, mean_loss)


def solution(mesh):
    return jax.shard_map(
        body,
        mesh=mesh,
        in_specs=(
            P(("grp", "fsdp", "item"), None, None),
            P(("grp", "fsdp", "item"), None),
            P(("grp", "fsdp", "item"), None),
            P(("grp", "fsdp", "item")),
            P(),
            P("fsdp", None),
            P(),
            P("item", None),
        ),
        out_specs=(P("fsdp", None), P(), P()),
        check_vma=False,
    )
```

profile of v0, /device:TPU:0, one launch (start us, length us, event | category | flops | bytes accessed | tf_op | source)
XLA Modules:
  0.0 467.6 jit_solution(16118268439128578263)
XLA Ops:
  7.2 0.7 all-gather.5.cloned.1.call-update
  7.9 0.7 all-gather.3.cloned.1.call-update
  8.7 0.7 convert_element_type.34
  9.4 0.7 convert_element_type.36
  10.1 0.7 compare_and_fusion.1
  11.0 0.7 compare_select_fusion
  11.9 5.1 %fusion = f32[64,16]{1,0:T(8,128)S(1)} fusion(bf16[64,16,4096]{2,1,0:T(8,128)(2,1)} %param.8), kind=kLoop, calls=%fused_computation.3 | loop fusion | flops 12581888 | bytes 8392704 | tf_op jit(solution)/shard_map/reduce_sum | solution.py:15
  17.0 78.3 %all-gather.5.cloned.1.call-done = bf16[4096,1024]{1,0:T(8,128)(2,1)} async-done(((bf16[1024,1024]{1,0:T(8,128)(2,1)}), bf16[4096,1024]{1,0:T(8,128)(2,1)}) %all-gather.5.cloned.1.call-update) | async-done | bytes 8388624 | tf_op jit(solution)/shard_map/all_gather | solution.py:117
  95.2 15.4 %gather_fusion = bf16[2048,1024]{1,0:T(8,128)(2,1)} fusion(bf16[4096,1024]{1,0:T(8,128)(2,1)} %all-gather.5.cloned.1.call-done, s32[2048]{0:T(1024)S(1)} %broadcast_clamp_fusion), kind=kCustom, calls=%fused_computation | custom fusion | bytes 8396800 | tf_op jit(solution)/shard_map/jit(_take)/gather | solution.py:119
  110.7 3.7 fusion.3
  114.4 57.0 %all-gather.3.cloned.1.call-done = bf16[4096,1024]{1,0:T(8,128)(2,1)} async-done(((bf16[256,1024]{1,0:T(8,128)(2,1)}), bf16[4096,1024]{1,0:T(8,128)(2,1)}) %all-gather.3.cloned.1.call-update) | async-done | bytes 8388624 | tf_op jit(solution)/shard_map/all_gather | solution.py:112
  171.4 12.9 %fusion.4 = f32[64,16,1024]{2,1,0:T(8,128)S(1)} fusion(bf16[4096,1024]{1,0:T(8,128)(2,1)} %all-gather.3.cloned.1.call-done, bf16[64,16,4096]{2,1,0:T(8,128)(2,1)} %param.8, f32[4096]{0:T(1024)S(1)} %convert_element_type.34, f32[64,16]{1,0:T(8,128)S(1)} %add_rsqrt_fusion), kind=kOutput, calls=%fused_computation.9 | convolution fusion | flops 8606711808 | bytes 20992000 | tf_op jit(solution)/shard_map/dot_general | solution.py:109
  184.3 1.9 copy-done
  186.2 14.7 %fusion.45 = f32[1,64,16]{2,0,1:T(1,128)S(1)} fusion(f32[64,16,1024]{2,1,0:T(8,128)S(1)} %fusion.4, f32[1024,1,1]{0,1,2:T(1,128)S(1)} %bitcast.90), kind=kOutput, calls=%fused_computation.79 | convolution fusion | flops 12582912 | bytes 4202496 | tf_op jit(solution)/shard_map/qsp,p->qs/dot_general | solution.py:24
  201.1 4.5 fusion.46
  205.6 0.1 fusion.18
  205.7 0.2 fusion.16
  206.0 2.1 fusion.9
  208.3 0.4 copy-done.7
  208.8 0.1 copy.31
  208.9 2.9 fusion.8
  211.8 0.3 fusion.20
  212.1 0.3 fusion.23
  212.4 4.8 %fusion.24 = f32[64,1,16]{2,1,0:T(1,128)S(1)} fusion(f32[64,16,1024]{2,1,0:T(8,128)S(1)} %copy-done.1, f32[64,1024,1]{1,0,2:T(8,128)S(1)} %bitcast.88), kind=kOutput, calls=%fused_computation.36 | convolution fusion | flops 12582912 | bytes 4460544 | tf_op jit(solution)/shard_map/qsp,qp->qs/dot_general | solution.py:93
  217.4 0.6 add_convert_fusion
  218.0 16.2 %convolution_bitcast_fusion = f32[4096,1024]{1,0:T(8,128)} fusion(bf16[64,16,4096]{2,1,0:T(8,128)(2,1)} %param.8, f32[4096]{0:T(1024)S(1)} %convert_element_type.34, f32[64,16]{1,0:T(8,128)S(1)} %add_rsqrt_fusion, bf16[64,16,1024]{2,0,1:T(8,128)(2,1)S(1)} %add_convert_fusion), kind=kOutput, calls=%fused_computation.6 | convolution fusion | flops 8606711808 | bytes 27283456 | tf_op jit(solution)/shard_map/dot_general | solution.py:131
  234.3 145.1 %reduce-scatter.2.cloned.1.call-done = f32[256,1024]{1,0:T(8,128)} async-done(((f32[4096,1024]{1,0:T(8,128)}), f32[256,1024]{1,0:T(8,128)}) %reduce-scatter.2.cloned.1.call-update) | async-done | bytes 1048592 | tf_op jit(solution)/shard_map/reduce_scatter | solution.py:130
  379.6 0.6 subtract_reduce_fusion
  380.2 3.9 fusion.47
  384.1 64.9 %all-reduce = (f32[1024]{0:T(1024)}, f32[]{:T(128)}) all-reduce(f32[1024]{0:T(1024)S(1)} %bitcast.91, f32[]{:T(128)} %subtract_reduce_fusion), channel_id=1, replica_groups=mesh['grp'=2,'fsdp'=16,'item'=4] {'grp','fsdp','item'}, use_global_device_ids=true, to_apply=%region_7.8 | all-reduce | flops 1025 | bytes 8200 | tf_op jit(solution)/shard_map/psum | solution.py:139
  449.6 8.0 %all-reduce.3.cloned.1.call-done = f32[256,1024]{1,0:T(8,128)} async-done(((f32[256,1024]{1,0:T(8,128)}), f32[256,1024]{1,0:T(8,128)}) %all-reduce.3.cloned.1.call-update) | async-done | bytes 1048592 | tf_op jit(solution)/shard_map/psum | solution.py:138
  457.7 2.3 copy.60
  (55 shorter events, 1.3 us)
Async XLA Ops:
  7.2 88.1 %all-gather.5.cloned.1.call-start = ((), (), s32[]{:S(2)}) async-start(), calls=%async_computation.2 | async-start | bytes 10485760 | tf_op jit(solution)/shard_map/all_gather | solution.py:117
  7.9 163.5 %all-gather.3.cloned.1.call-start = ((), (), s32[]{:S(2)}) async-start(), calls=%async_computation.1 | async-start | bytes 8912896 | tf_op jit(solution)/shard_map/all_gather | solution.py:112
  8.6 370.8 %reduce-scatter.2.cloned.1.call-start = ((), (), s32[]{:S(2)}) async-start(), calls=%async_computation.3 | async-start | bytes 17825792 | tf_op jit(solution)/shard_map/reduce_scatter | solution.py:130
  114.4 71.8 %copy-start.6 = (f32[1024]{0:T(1024)S(1)}, f32[1024]{0:T(1024)}, u32[]{:S(2)}) copy-start(f32[1024]{0:T(1024)} %param.14) | copy-start | bytes 12292
  184.3 1.9 copy-start
  184.3 16.7 %copy-start.9 = (s32[64]{0:T(128)S(1)}, s32[64]{0:T(128)}, u32[]{:S(2)}) copy-start(s32[64]{0:T(128)} %param.11) | copy-start | bytes 772
  186.2 19.5 %copy-start.3 = (bf16[64,1024]{1,0:T(8,128)(2,1)S(1)}, bf16[64,1024]{1,0:T(8,128)(2,1)}, u32[]{:S(2)}) copy-start(bf16[64,1024]{1,0:T(8,128)(2,1)} %param.9) | copy-start | bytes 393220
  201.1 4.9 %copy-start.2 = (bf16[2048,1024]{1,0:T(8,128)(2,1)S(1)}, bf16[2048,1024]{1,0:T(8,128)(2,1)}, u32[]{:S(2)}) copy-start(bf16[2048,1024]{1,0:T(8,128)(2,1)} %gather_fusion) | copy-start | bytes 12582916
  206.0 2.2 copy-start.12
  206.0 2.4 copy-start.10
  208.2 0.5 copy-start.7
  208.9 3.5 copy-start.1
  217.4 16.8 %copy-start.4 = (f32[64,16]{0,1:T(8,128)}, f32[64,16]{0,1:T(8,128)S(1)}, u32[]{:S(2)}) copy-start(f32[64,16]{0,1:T(8,128)S(1)} %fusion.32) | copy-start | bytes 12292
  234.2 145.3 %copy-start.5 = (f32[64,16]{0,1:T(8,128)S(1)}, f32[64,16]{0,1:T(8,128)}, u32[]{:S(2)}) copy-start(f32[64,16]{0,1:T(8,128)} %copy-done.4) | copy-start | bytes 12292
  234.2 145.4 %copy-start.8 = (f32[64]{0:T(128)S(1)}, f32[64]{0:T(128)}, u32[]{:S(2)}) copy-start(f32[64]{0:T(128)} %copy-done.7) | copy-start | bytes 772
  234.2 145.4 %copy-start.11 = (f32[64]{0:T(128)S(1)}, f32[64]{0:T(128)}, u32[]{:S(2)}) copy-start(f32[64]{0:T(128)} %copy-done.10) | copy-start | bytes 772
  234.2 145.4 %copy-start.13 = (f32[64]{0:T(128)S(1)}, f32[64]{0:T(128)}, u32[]{:S(2)}) copy-start(f32[64]{0:T(128)} %copy-done.12) | copy-start | bytes 772
  234.3 223.4 %all-reduce.3.cloned.1.call-start = ((), (), s32[]{:S(2)}) async-start(), calls=%async_computation.4 | async-start | bytes 2097152 | tf_op jit(solution)/shard_map/psum | solution.py:138
Sparse Core Ops, SparseCore 0:
  9.6 85.5 all-gather.4
  97.6 73.7 all-gather.2
  234.4 145.0 reduce-scatter.1
  381.8 75.8 all-reduce.2
where the time goes:
time: 468 us
  waiting for transfers between devices  290 us (62%)
  blocking collectives  64.9 us (14%)
  matrix products  62 us (13%)
  local copies, waits for them, and re-layouts  21 us (4%)
  between operations  15.8 us (3%)
  other arithmetic  14 us (3%)
    reduce_scatter x1, waiting for transfers between devices, body(): lax.psum_scatter(lax.dot_general(normed, grad_tokens, (((0,), (0,)), ((),...  145 us
    all_gather x1, waiting for transfers between devices, body(): slab_piece = lax.all_gather(slab, 'item', axis=0, tiled=True)  78.3 us
    psum x1, blocking collectives, body(): lax.psum((query_part, loss_part), ('grp', 'fsdp', 'item'))  64.9 us
    all_gather x1, waiting for transfers between devices, project(): return add_rows(lax.all_gather(proj_weight, 'fsdp', axis=0, tiled=True))  57 us
    dot_general x1, matrix products, body(): lax.dot_general(normed, grad_tokens, (((0,), (0,)), ((), ())), preferred_...  16.2 us
    gather x1, local copies, waits for them, and re-layouts, body(): jnp.take(slab_piece, jnp.clip(negatives, 0, slab_piece.shape[0] - 1), axi...  15.4 us
    dot_general x1, matrix products, gated_pool(): jnp.einsum('qsp,p->qs', tokens, pool_query, precision=lax.Precision.HIGHEST)  14.7 us
    dot_general x1, matrix products, add_rows(): return jnp.dot(normed, shard_rows, preferred_element_type=jnp.float32)  12.9 us
  transfers between devices with their start and end apart: 4, of which 4 were waited for; matrix products, arithmetic and copies ran while one was open for 7% of the time, Pallas kernels for 0%

commit v1 on v0

v1 whole, which is shorter than its diff:
```python
import functools
import math

import jax
import jax.numpy as jnp
from jax import lax
from jax.experimental import pallas as pl
from jax.experimental.pallas import tpu as pltpu
from jax.sharding import PartitionSpec as P

MESH = pl.DeviceIdType.MESH
BF = jnp.bfloat16
F32 = jnp.float32
TEMP = 0.05
NORM_EPS = 1e-5
EMB_EPS = 1e-6

COLX = (0, 128)
COLY = (128, 256)
COLZ = (384, 128)

N_SEM = 112


def dev(x, y, z, c):
    return (lax.rem(z, 2), x * 4 + (z // 2) * 2 + c, y)


def mo(v, m):
    return pl.multiple_of(v, m)


def split2(v):
    hi = v.astype(BF)
    lo = (v - hi.astype(F32)).astype(BF)
    return hi, lo


def col_to_row(v, n):
    return jnp.transpose(jnp.broadcast_to(v, (n, 128)))[0:1, :]


def kernel(
    h_ref, pos_ref, neg_ref, wt_ref, gain_ref, w_ref, pq_ref, slab_ref,
    out_ref, gq_ref, loss_ref,
    XN, WO, WH, V, SLAB, SCR, NG, CM, LG, AT, NB, ACC, PO, EA, WB, GS, GR, DS, DR,
    GP, NTS, NTR, GA, PA, PBS, PBR, PCS, PCR, PG, OG, UP, UR, SACC, Z, ZR, GQ,
    ss, rs, hs, ls,
):
    g_i = lax.axis_index("grp")
    f_i = lax.axis_index("fsdp")
    y = lax.axis_index("item")
    x = f_i // 4
    zh = lax.rem(f_i // 2, 2)
    c = lax.rem(f_i, 2)
    z = zh * 2 + g_i
    zl = g_i
    zf = 3 - z
    oc = 1 - c

    def xs(d):
        return lax.rem(x + d, 4)

    def ys(d):
        return lax.rem(y + d, 4)

    def zs(d):
        return lax.rem(z + d, 4)

    hcp = []
    for i in range(8):
        cp = pltpu.make_async_copy(
            h_ref.at[pl.ds(i * 128, 128)], XN.at[pl.ds(i * 128, 128)], hs.at[i]
        )
        hcp.append(cp)
    own_w = pltpu.make_async_copy(
        w_ref.at[:, pl.ds(mo(c * 512, 512), 512)], WO.at[c], ls.at[0]
    )
    slab_cp = pltpu.make_async_copy(slab_ref, SLAB, ls.at[1])
    own_w.start()
    hcp[0].start()

    peers = []
    for dx in range(4):
        for fl in range(2):
            for dc in range(2):
                if (dx, fl, dc) != (0, 0, 0):
                    peers.append(dev(xs(dx), y, zf if fl else z, oc if dc else c))
    for d in (1, 2, 3):
        peers.append(dev(x, ys(d), z, c))
    zg = zh * 2 + (1 - zl)
    zo = 3 - zg
    for zz in (zg, zo):
        peers.append(dev(x, y, zz, c))
    for d in (1, 2, 3):
        peers.append(dev(x, ys(d), zg, c))
    bar = pltpu.get_barrier_semaphore()
    for p in peers:
        pl.semaphore_signal(bar, inc=1, device_id=p, device_id_type=MESH)
    pl.semaphore_wait(bar, len(peers))

    started = []

    def send(src, dst, to):
        k = len(started)
        cp = pltpu.make_async_remote_copy(
            src_ref=src, dst_ref=dst, send_sem=ss.at[k], recv_sem=rs.at[k],
            device_id=to, device_id_type=MESH,
        )
        cp.start()
        started.append(cp)
        return cp

    def recv(cps):
        for cp in cps:
            cp.wait_recv()

    sib = dev(x, y, z, oc)
    k_w = send(w_ref.at[:, pl.ds(mo(oc * 512, 512), 512)], WO.at[c], sib)
    for i in range(1, 8):
        hcp[i].start()
    slab_cp.start()
    k_neg = [
        send(neg_ref.at[ys(d)], NG.at[y], dev(x, ys(d), z, c)) for d in (1, 2, 3)
    ]
    NG[y] = neg_ref[y]

    wf = jnp.sum(w_ref[...].astype(F32) * pq_ref[...], axis=1, keepdims=True)
    vcol = mo(f_i * 256, 256)
    V[:, pl.ds(vcol, 256)] = col_to_row(wf, 256)
    k_v = []
    for dx in range(4):
        for fl in range(2):
            for dc in range(2):
                if (dx, fl, dc) != (0, 0, 0):
                    k_v.append(
                        send(
                            V.at[:, pl.ds(vcol, 256)], V.at[:, pl.ds(vcol, 256)],
                            dev(xs(dx), y, zf if fl else z, oc if dc else c),
                        )
                    )

    own_w.wait()
    k_w.wait_recv()
    cx = pl.ds(*COLX)
    cy = pl.ds(*COLY)
    cz = pl.ds(*COLZ)
    wo5 = WO.reshape(2, 2, 4, 32, 512)
    k_xp = send(wo5.at[:, :, :, :, cx], WH.at[x, zh, :, :, :, :, cx], dev(x, y, zf, c))
    k_yp = []
    for dx in range(4):
        for fl in range(2):
            if (dx, fl) != (0, 0):
                k_yp.append(
                    send(
                        wo5.at[:, :, y, :, cy], WH.at[x, zh, :, :, y, :, cy],
                        dev(xs(dx), y, zf if fl else z, c),
                    )
                )
    k_zp = [
        send(
            wo5.at[:, zl, :, :, cz], WH.at[x, zh, :, zl, :, :, cz], dev(xs(d), y, z, c)
        )
        for d in (1, 2, 3)
    ]
    k_xm = [
        send(wo5.at[:, :, :, :, cx], WH.at[x, zh, :, :, :, :, cx], dev(xs(d), y, z, c))
        for d in (1, 2, 3)
    ]
    for ci in range(2):
        for a in range(2):
            WH[x, zh, ci, a, :, :, cx] = wo5[ci, a, :, :, cx]
            WH[x, zh, ci, a, y, :, cy] = wo5[ci, a, y, :, cy]
        WH[x, zh, ci, zl, :, :, cz] = wo5[ci, zl, :, :, cz]

    def norm_rows(i, carry):
        r = pl.ds(mo(i * 16, 16), 16)
        ms = jnp.zeros((16, 128), F32)
        for j in range(8):
            xv = XN[r, j * 512 : (j + 1) * 512].astype(F32)
            sq = xv * xv
            ms = ms + ((sq[:, 0:128] + sq[:, 128:256]) + (sq[:, 256:384] + sq[:, 384:512]))
        inv = lax.rsqrt(jnp.sum(ms, axis=1, keepdims=True) / 4096.0 + NORM_EPS)
        for j in range(8):
            cs = slice(j * 512, (j + 1) * 512)
            XN[r, cs] = (
                XN[r, cs].astype(F32) * inv * gain_ref[:, cs].astype(F32)
            ).astype(BF)
        return carry

    for i in range(2):
        hcp[i].wait()
        lax.fori_loop(i * 8, i * 8 + 8, norm_rows, 0, unroll=2)

    k_xp.wait_recv()
    k_xm2 = [
        send(
            WH.at[x, 1 - zh, :, :, :, :, cx], WH.at[x, 1 - zh, :, :, :, :, cx],
            dev(xs(d), y, z, c),
        )
        for d in (1, 2, 3)
    ]
    recv(k_zp)
    k_zm = [
        send(
            WH.at[:, zh, :, zl, :, :, cz], WH.at[:, zh, :, zl, :, :, cz],
            dev(x, y, zs(d), c),
        )
        for d in (1, 2, 3)
    ]
    recv(k_yp)
    k_ym = [
        send(WH.at[:, :, :, :, y, :, cy], WH.at[:, :, :, :, y, :, cy], dev(x, ys(d), z, c))
        for d in (1, 2, 3)
    ]

    for i in range(2, 8):
        hcp[i].wait()
        lax.fori_loop(i * 8, i * 8 + 8, norm_rows, 0, unroll=2)

    recv(k_v)

    def gate_rows(i, carry):
        r = pl.ds(mo(i * 16, 16), 16)
        acc = jnp.zeros((16, 128), F32)
        for j in range(8):
            cs = slice(j * 512, (j + 1) * 512)
            p = XN[r, cs].astype(F32) * V[:, cs]
            acc = acc + ((p[:, 0:128] + p[:, 128:256]) + (p[:, 256:384] + p[:, 384:512]))
        LG[r, :] = jnp.broadcast_to(jnp.sum(acc, axis=1, keepdims=True), (16, 128))
        return carry

    lax.fori_loop(0, 64, gate_rows, 0, unroll=2)

    def at_rows(i, carry):
        r = pl.ds(mo(i * 256, 256), 256)
        gate = jax.nn.sigmoid(LG[r, :] * (1.0 / 32.0))
        LG[r, :] = gate
        wg = gate * wt_ref[r, :]
        q = (lax.broadcasted_iota(jnp.int32, (256, 128), 0) + i * 256) // 16
        lane = lax.broadcasted_iota(jnp.int32, (256, 128), 1)
        hi = wg.astype(BF).astype(F32)
        a = jnp.where(lane == q, hi, 0.0) + jnp.where(lane == q + 64, wg - hi, 0.0)
        AT[:, r] = jnp.transpose(a).astype(BF)
        return carry

    lax.fori_loop(0, 4, at_rows, 0)

    qrow = mo(c * 64, 64)

    def n_cols(i, carry):
        cs = pl.ds(mo(i * 512, 512), 512)
        rr = jnp.dot(AT[...], XN[:, cs], preferred_element_type=F32)
        hi, lo = split2(rr[:64] + rr[64:])
        NB[0, pl.ds(qrow, 64), cs] = hi
        NB[1, pl.ds(qrow, 64), cs] = lo
        return carry

    lax.fori_loop(0, 8, n_cols, 0)
    k_n = send(NB.at[:, pl.ds(qrow, 64), :], NB.at[:, pl.ds(qrow, 64), :], sib)

    slab_cp.wait()
    for i in range(4):
        sv = SLAB[i * 256 : (i + 1) * 256, :].astype(F32)
        sm = lax.rsqrt(jnp.sum(sv * sv, axis=1, keepdims=True) / 1024.0 + EMB_EPS)
        SCR[:, i * 256 : (i + 1) * 256] = col_to_row(sm * (1.0 / (32.0 * TEMP)), 256)
    recv(k_neg)

    def count_rows(i, carry):
        src = i // 4
        r = pl.ds(mo(lax.rem(i, 4) * 16, 16), 16)
        ids = NG[src, r, :] - y * 1024
        row = lax.broadcasted_iota(jnp.int32, (16, 1024), 1)
        cnt = jnp.zeros((16, 1024), F32)
        for k in range(8):
            cnt = cnt + jnp.where(row == ids[:, k : k + 1], 1.0, 0.0)
        CM[pl.ds(mo(i * 16, 16), 16), :] = cnt
        return carry

    lax.fori_loop(0, 16, count_rows, 0)

    k_n.wait_recv()

    def nt_block(i, carry):
        xi = i // 2
        zi = lax.rem(i, 2)
        cs = pl.ds(mo(xi * 1024 + zi * 512 + c * 256, 256), 256)
        for p in range(2):
            NTS[xi, p, pl.ds(mo(zi * 256, 256), 256), :] = jnp.transpose(
                NB[p, :, cs].astype(F32)
            ).astype(BF)
        return carry

    lax.fori_loop(0, 8, nt_block, 0)

    recv(k_xm)
    recv(k_xm2)
    recv(k_zm)
    recv(k_ym)
    k_nt = [send(NTS.at[xs(d)], NTR.at[d - 1], dev(xs(d), y, z, c)) for d in (1, 2, 3)]

    ACC[...] = jnp.zeros_like(ACC)

    def pool_k(k, carry):
        w = WH[k // 4, lax.rem(k // 2, 2), lax.rem(k, 2)].reshape(256, 512)
        a = NB[:, :, pl.ds(mo(k * 256, 256), 256)].reshape(256, 256)
        ACC[...] += jnp.dot(a, w, preferred_element_type=F32)
        return carry

    lax.fori_loop(0, 16, pool_k, 0)
    orow = mo(oc * 64, 64)
    PO[c] = ACC[pl.ds(qrow, 64), :] + ACC[pl.ds(128 + qrow, 64), :]
    PO[2 + c] = ACC[pl.ds(orow, 64), :] + ACC[pl.ds(128 + orow, 64), :]
    k_po = send(PO.at[2 + c], PO.at[c], sib)
    k_po.wait_recv()
    pooled = jnp.concatenate([PO[0], PO[1]], axis=1)
    mean_sq = jnp.mean(pooled * pooled, axis=1, keepdims=True)
    unit = lax.rsqrt(mean_sq + EMB_EPS) / 32.0
    emb = (pooled * unit).astype(BF)
    EA[y] = emb
    k_e = [send(EA.at[y], EA.at[y], dev(x, ys(d), z, c)) for d in (1, 2, 3)]

    posf = pos_ref[...].astype(F32)
    pm = lax.rsqrt(jnp.mean(posf * posf, axis=1, keepdims=True) + EMB_EPS) * (
        1.0 / (32.0 * TEMP)
    )
    ps = jnp.sum(emb.astype(F32) * posf, axis=1, keepdims=True) * pm
    pe = jnp.exp(ps)

    recv(k_e)
    ea = EA[...].reshape(256, 1024)
    den = jnp.zeros((256, 1), F32)
    for i in range(4):
        cs = slice(i * 256, (i + 1) * 256)
        s = lax.dot_general(
            ea, SLAB[cs, :], (((1,), (1,)), ((), ())), preferred_element_type=F32
        )
        ew = jnp.exp(s * SCR[:, cs]) * CM[:, cs]
        den = den + jnp.sum(ew, axis=1, keepdims=True)
        WB[:, cs] = (ew * SCR[:, cs]).astype(BF)
    DS[...] = jnp.broadcast_to(den, (256, 128)).reshape(4, 64, 128)
    k_d = [send(DS.at[ys(d)], DR.at[d - 1], dev(x, ys(d), z, c)) for d in (1, 2, 3)]
    for i in range(2):
        cs = slice(i * 512, (i + 1) * 512)
        GS[:, :, cs] = (
            jnp.dot(WB[...], SLAB[:, cs], preferred_element_type=F32)
            .reshape(4, 64, 512)
            .astype(BF)
        )
    k_g = [send(GS.at[ys(d)], GR.at[d - 1], dev(x, ys(d), z, c)) for d in (1, 2, 3)]
    recv(k_d)
    denom = pe + (DS[y] + DR[0] + DR[1] + DR[2])[:, 0:1]
    rden = 1.0 / denom
    loss = jnp.sum(jnp.log(denom) - ps, axis=0, keepdims=True)
    Z[0, :, 4096:4224] = jnp.broadcast_to(loss, (1, 128))
    recv(k_g)
    gsum = (
        GS[y].astype(F32) + GR[0].astype(F32) + GR[1].astype(F32) + GR[2].astype(F32)
    )
    g_emb = (pe * rden - 1.0) * pm * posf + gsum * rden
    radial = jnp.sum(pooled * g_emb, axis=1, keepdims=True)
    g_pool = unit * g_emb - pooled * (radial * unit / (1024.0 * (mean_sq + EMB_EPS)))
    hi, lo = split2(g_pool)
    GP[0, pl.ds(qrow, 64), :] = hi
    GP[1, pl.ds(qrow, 64), :] = lo
    k_gp = send(GP.at[:, pl.ds(qrow, 64), :], GP.at[:, pl.ds(qrow, 64), :], sib)
    k_gp.wait_recv()

    k_ga = [send(GP.at[0], GA.at[d - 1], dev(xs(d), y, z, c)) for d in (1, 2, 3)]

    gph = GP[:, :, pl.ds(mo(c * 512, 512), 512)].reshape(256, 512)

    def u_block(k, carry):
        w = WH[k // 4, lax.rem(k // 2, 2), lax.rem(k, 2)].reshape(256, 512)
        u = lax.dot_general(gph, w, (((1,), (1,)), ((), ())), preferred_element_type=F32)
        UP[:, pl.ds(mo(k * 256, 256), 256)] = u[:128] + u[128:]
        return carry

    lax.fori_loop(0, 16, u_block, 0)
    k_u = send(UP.at[pl.ds(orow, 64), :], UR, sib)

    recv(k_nt)
    PA[...] = jnp.dot(NTS[x, 0], GP[0], preferred_element_type=F32) + jnp.dot(
        NTS[x, 1], GP[0], preferred_element_type=F32
    )
    recv(k_ga)

    def fac(i, carry):
        PA[...] += jnp.dot(NTR[i, 0], GA[i], preferred_element_type=F32) + jnp.dot(
            NTR[i, 1], GA[i], preferred_element_type=F32
        )
        return carry

    lax.fori_loop(0, 3, fac, 0)
    PBS[...] = PA[...].astype(BF).reshape(4, 128, 1024)
    k_pb = [send(PBS.at[zs(d)], PBR.at[d - 1], dev(x, y, zs(d), c)) for d in (1, 2, 3)]

    k_u.wait_recv()
    SACC[...] = jnp.zeros_like(SACC)

    def slope_rows(i, carry):
        r = pl.ds(mo(i * 16, 16), 16)
        uo = pl.ds(qrow + i, 1)
        acc = jnp.zeros((16, 128), F32)
        for j in range(8):
            cs = slice(j * 512, (j + 1) * 512)
            u = UP[uo, cs] + UR[pl.ds(i, 1), cs]
            p = XN[r, cs].astype(F32) * u
            acc = acc + ((p[:, 0:128] + p[:, 128:256]) + (p[:, 256:384] + p[:, 384:512]))
        pd = jnp.sum(acc, axis=1, keepdims=True)
        gate = LG[r, 0:1]
        slope = wt_ref[r, :] * gate * (1.0 - gate) * pd * (1.0 / 32.0)
        for j in range(8):
            cs = slice(j * 512, (j + 1) * 512)
            SACC[:, cs] += XN[r, cs].astype(F32) * slope
        return carry

    lax.fori_loop(0, 64, slope_rows, 0, unroll=2)
    Z[0, :, 0:4096] = jnp.sum(SACC[...], axis=0, keepdims=True)
    ZR[0, c] = Z[0]
    k_z0 = send(Z.at[0], ZR.at[0, c], sib)

    recv(k_pb)
    zrow = mo(z * 128, 128)
    pc = PA[pl.ds(zrow, 128), :] + (
        PBR[0].astype(F32) + PBR[1].astype(F32) + PBR[2].astype(F32)
    )
    PA[0:128, :] = pc
    PCS[...] = pc.astype(BF).reshape(4, 32, 1024)
    k_pc = [send(PCS.at[ys(d)], PCR.at[d - 1], dev(x, ys(d), z, c)) for d in (1, 2, 3)]

    k_z0.wait_recv()
    Z[1] = ZR[0, 0] + ZR[0, 1]
    ZR[1, x] = Z[1]
    k_z1 = [send(Z.at[1], ZR.at[1, x], dev(xs(d), y, z, c)) for d in (1, 2, 3)]

    recv(k_pc)
    piece = PA[pl.ds(mo(y * 32, 32), 32), :] + (
        PCR[0].astype(F32) + PCR[1].astype(F32) + PCR[2].astype(F32)
    )
    PG[...] = piece.astype(BF)
    OG[zl, y] = PG[...]
    k_og = [send(PG, OG.at[zl, y], dev(x, ys(d), z, c)) for d in (1, 2, 3)]
    k_og += [send(PG, OG.at[zl, y], dev(x, ys(d), zg, c)) for d in range(4)]

    recv(k_z1)
    Z[2] = (ZR[1, 0] + ZR[1, 1]) + (ZR[1, 2] + ZR[1, 3])
    ZR[2, y] = Z[2]
    k_z2 = [send(Z.at[2], ZR.at[2, y], dev(x, ys(d), z, c)) for d in (1, 2, 3)]
    recv(k_z2)
    Z[3] = (ZR[2, 0] + ZR[2, 1]) + (ZR[2, 2] + ZR[2, 3])
    ZR[3, z] = Z[3]
    k_z3 = [send(Z.at[3], ZR.at[3, z], dev(x, y, zs(d), c)) for d in (1, 2, 3)]
    recv(k_z3)
    tot = (ZR[3, 0] + ZR[3, 1]) + (ZR[3, 2] + ZR[3, 3])
    Z[4] = tot
    loss_ref[...] = Z[4, :, 4096:4224] * (1.0 / 8192.0)

    row16 = lax.broadcasted_iota(jnp.int32, (16, 256), 0)
    ACC[0:16, :] = jnp.zeros((16, 512), F32)

    def gq_k(k, carry):
        w = WH[k // 4, lax.rem(k // 2, 2), lax.rem(k, 2)].reshape(256, 512)
        sv = Z[4, :, pl.ds(mo(k * 256, 256), 256)]
        h1 = sv.astype(BF).astype(F32)
        r1 = sv - h1
        h2 = r1.astype(BF).astype(F32)
        a = jnp.where(row16 == 0, h1, jnp.where(row16 == 1, h2, jnp.where(row16 == 2, r1 - h2, 0.0)))
        ACC[0:16, :] += jnp.dot(a.astype(BF), w, preferred_element_type=F32)
        return carry

    lax.fori_loop(0, 16, gq_k, 0)
    GQ[c] = jnp.sum(ACC[0:16, :], axis=0, keepdims=True)
    k_gq = send(GQ.at[c], GQ.at[c], sib)

    s_blk = Z[4, :, pl.ds(vcol, 256)]
    s_col = jnp.transpose(jnp.broadcast_to(s_blk, (128, 256)))[:, 0:1]
    recv(k_og)
    og = OG[...].reshape(256, 1024).astype(F32)
    out_ref[...] = og + s_col * pq_ref[...]
    k_gq.wait_recv()
    gq_ref[:, 0:512] = GQ[0]
    gq_ref[:, 512:1024] = GQ[1]

    for cp in started:
        cp.wait_send()


def body(hidden_states, positives, negatives, lengths, norm_gain, proj_weight, pool_query, slab):
    lists = jnp.transpose(negatives.reshape(64, 4, 8), (1, 0, 2))
    lists = jnp.pad(lists, ((0, 0), (0, 0), (0, 120)), constant_values=-1)
    slot = lax.broadcasted_iota(jnp.int32, (64, 16), 1)
    wt = jnp.where(slot < lengths[:, None], 1.0, 0.0).astype(F32) / lengths[:, None].astype(F32)
    vm = pl.BlockSpec(memory_space=pltpu.VMEM)
    anyspace = pl.BlockSpec(memory_space=pl.ANY)
    scratch = [
        pltpu.VMEM((1024, 4096), BF),
        pltpu.VMEM((2, 256, 512), BF),
        pltpu.VMEM((4, 2, 2, 2, 4, 32, 512), BF),
        pltpu.VMEM((1, 4096), F32),
        pltpu.VMEM((1024, 1024), BF),
        pltpu.VMEM((1, 1024), F32),
        pltpu.VMEM((4, 64, 128), jnp.int32),
        pltpu.VMEM((256, 1024), F32),
        pltpu.VMEM((1024, 128), F32),
        pltpu.VMEM((128, 1024), BF),
        pltpu.VMEM((2, 128, 4096), BF),
        pltpu.VMEM((256, 512), F32),
        pltpu.VMEM((4, 64, 512), F32),
        pltpu.VMEM((4, 64, 1024), BF),
        pltpu.VMEM((256, 1024), BF),
        pltpu.VMEM((4, 64, 1024), BF),
        pltpu.VMEM((3, 64, 1024), BF),
        pltpu.VMEM((4, 64, 128), F32),
        pltpu.VMEM((3, 64, 128), F32),
        pltpu.VMEM((2, 128, 1024), BF),
        pltpu.VMEM((4, 2, 512, 128), BF),
        pltpu.VMEM((3, 2, 512, 128), BF),
        pltpu.VMEM((3, 128, 1024), BF),
        pltpu.VMEM((512, 1024), F32),
        pltpu.VMEM((4, 128, 1024), BF),
        pltpu.VMEM((3, 128, 1024), BF),
        pltpu.VMEM((4, 32, 1024), BF),
        pltpu.VMEM((3, 32, 1024), BF),
        pltpu.VMEM((32, 1024), BF),
        pltpu.VMEM((2, 4, 32, 1024), BF),
        pltpu.VMEM((128, 4096), F32),
        pltpu.VMEM((64, 4096), F32),
        pltpu.VMEM((16, 4096), F32),
        pltpu.VMEM((5, 1, 4224), F32),
        pltpu.VMEM((4, 4, 1, 4224), F32),
        pltpu.VMEM((2, 1, 512), F32),
        pltpu.SemaphoreType.DMA((N_SEM,)),
        pltpu.SemaphoreType.DMA((N_SEM,)),
        pltpu.SemaphoreType.DMA((8,)),
        pltpu.SemaphoreType.DMA((2,)),
    ]
    grad, gq, loss = pl.pallas_call(
        kernel,
        out_shape=(
            jax.ShapeDtypeStruct((256, 1024), F32),
            jax.ShapeDtypeStruct((1, 1024), F32),
            jax.ShapeDtypeStruct((1, 128), F32),
        ),
        in_specs=[anyspace, vm, vm, vm, vm, vm, vm, anyspace],
        out_specs=(vm, vm, vm),
        scratch_shapes=scratch,
        compiler_params=pltpu.CompilerParams(
            collective_id=0, has_side_effects=True, vmem_limit_bytes=60 * 2**20
        ),
    )(
        hidden_states.reshape(1024, 4096), positives, lists, wt.reshape(1024, 1),
        norm_gain.reshape(1, 4096), proj_weight, pool_query.reshape(1, 1024), slab,
    )
    return grad, gq.reshape(1024), loss[0, 0]


def solution(mesh):
    return jax.shard_map(
        body,
        mesh=mesh,
        in_specs=(
            P(("grp", "fsdp", "item"), None, None),
            P(("grp", "fsdp", "item"), None),
            P(("grp", "fsdp", "item"), None),
            P(("grp", "fsdp", "item")),
            P(),
            P("fsdp", None),
            P(),
            P("item", None),
        ),
        out_specs=(P("fsdp", None), P(), P()),
        check_vma=False,
    )
```

time: 468 us -> 138 us (0.29)
  waiting for transfers between devices: 290 us -> 0 us
  Pallas kernels: 0 us -> 125 us
  blocking collectives: 64.9 us -> 0 us
  matrix products: 62 us -> 0 us
  local copies, waits for them, and re-layouts: 21 us -> 7.44 us
  between operations: 15.8 us -> 2.42 us
  other arithmetic: 14 us -> 1.4 us
    reduce_scatter x1 -> x0, waiting for transfers between devices: 145 us -> none  [body(): lax.psum_scatter(lax.dot_general(normed, grad_tokens, (((0,), (0,)), ((),...]
    all_gather x2 -> x0, waiting for transfers between devices: 135 us -> none  [the longest x1 78.3 us: body(): slab_piece = lax.all_gather(slab, 'item', axis=0, tiled=True)]
    pallas_call x0 -> x1, Pallas kernels: none -> 125 us  [body(): pl.pallas_call(kernel, out_shape=(jax.ShapeDtypeStruct((256, 1024), F32),...]
    psum x1 -> x0, blocking collectives: 64.9 us -> none  [body(): lax.psum((query_part, loss_part), ('grp', 'fsdp', 'item'))]
    dot_general x8 -> x0, matrix products: 62 us -> none  [the longest x1 16.2 us: body(): lax.dot_general(normed, grad_tokens, (((0,), (0,)), ((), ())), preferred_...]
    gather x1 -> x0, local copies, waits for them, and re-layouts: 15.4 us -> none  [body(): jnp.take(slab_piece, jnp.clip(negatives, 0, slab_piece.shape[0] - 1), axi...]
    psum x1 -> x0, waiting for transfers between devices: 8.04 us -> none  [body(): grad_proj = lax.psum(grad_shard, ('grp', 'item'))]
    reduce_sum x6 -> x0, other arithmetic: 6.37 us -> none  [the longest x1 5.08 us: normalize(): jnp.mean(flat_states * flat_states, axis=1, keepdims=True) + norm_eps]
  transfers between devices with their start and end apart: 4 -> 0, of which waited for: 4 -> 0; matrix products, arithmetic and copies ran while one was open for 7% -> 0% of each run, Pallas kernels for 0% -> 0%
where the time goes in v1:
time: 138 us; the launch traced here: 137 us
  Pallas kernels  125 us (91%)
  local copies, waits for them, and re-layouts  7.44 us (5%)
  between operations  2.42 us (2%)
  other arithmetic  1.4 us (1%)
    pallas_call x1, Pallas kernels, body(): pl.pallas_call(kernel, out_shape=(jax.ShapeDtypeStruct((256, 1024), F32),...  125 us
    unnamed x2, local copies, waits for them, and re-layouts  3.57 us

profile of v1, /device:TPU:0, one launch (start us, length us, event | category | flops | bytes accessed | tf_op | source)
XLA Modules:
  0.0 136.7 jit_solution(17586735436314297611)
XLA Ops:
  0.6 0.7 convert_element_type.4
  1.3 1.3 reshape.68.gain_ref
  2.6 0.7 select_divide_fusion
  3.3 0.8 copy.11
  4.1 0.7 pad.4.neg_ref
  4.8 1.1 div.21.wt_ref
  5.9 125.5 %shard_map.103 = (f32[256,1024]{1,0:T(8,128)}, f32[1,1024]{1,0:T(1,128)}, f32[1,128]{1,0:T(1,128)}) custom-call(bf16[1024,4096]{1,0:T(8,128)(2,1)} %bitcast.7, bf16[64,1024]{1,0:T(8,128)(2,1)} %pos_ref.1, s32[4,64,128]{2,1,0:T(8,128)} %pad.4.neg_ref, f32[1024,1]{1,0:T(8,128)} %div.21.wt_ref, bf16[1,4096]{1,0:T(2,128)(2,1)} %reshape.68.gain_ref, ...), custom_call_target="tpu_custom_call" | custom-call | tf_op jit(solution)/shard_map/pallas_call | solution.py:538
  131.4 2.3 %copy.16 = f32[256,1024]{1,0:T(8,128)} copy(f32[256,1024]{1,0:T(8,128)} %get-tuple-element.12) | data formatting | bytes 2097152
  133.7 1.3 copy.17

commit v2 on v1

v2 whole, which is shorter than its diff:
```python
import functools
import math

import jax
import jax.numpy as jnp
from jax import lax
from jax.experimental import pallas as pl
from jax.experimental.pallas import tpu as pltpu
from jax.sharding import PartitionSpec as P

MESH = pl.DeviceIdType.MESH
BF = jnp.bfloat16
F32 = jnp.float32
TEMP = 0.05
NORM_EPS = 1e-5
EMB_EPS = 1e-6

COLX = (0, 128)
COLY = (128, 256)
COLZ = (384, 128)

N_SEM = 112


def dev(x, y, z, c):
    return (lax.rem(z, 2), x * 4 + (z // 2) * 2 + c, y)


def mo(v, m):
    return pl.multiple_of(v, m)


def split2(v):
    hi = v.astype(BF)
    lo = (v - hi.astype(F32)).astype(BF)
    return hi, lo


def col_to_row(v, n):
    return jnp.transpose(jnp.broadcast_to(v, (n, 128)))[0:1, :]


def kernel(
    h_ref, pos_ref, neg_ref, len_ref, gain_ref, w_ref, pq1_ref, slab_ref,
    out_ref, sblk_ref, zt_ref,
    XN, WO, WH, V, SLAB, SCR, TN, NG, CM, LG, WT, GN, AT, NB, ACC, PO, EA, WB, GS, GR, DS, DR,
    GP, NT, NTX, NTZ, GAX, GAZ, PT, PA, PBS, PBR, PCS, PCR, PG, OG, UP, UR, SACC, Z, ZR, GQ,
    ss, rs, hs, ls,
):
    g_i = lax.axis_index("grp")
    f_i = lax.axis_index("fsdp")
    y = lax.axis_index("item")
    x = f_i // 4
    zh = lax.rem(f_i // 2, 2)
    c = lax.rem(f_i, 2)
    z = zh * 2 + g_i
    zl = g_i
    zf = 3 - z
    oc = 1 - c

    def xs(d):
        return lax.rem(x + d, 4)

    def ys(d):
        return lax.rem(y + d, 4)

    def zs(d):
        return lax.rem(z + d, 4)

    pq = pq1_ref[...].reshape(1, 1024)
    hcp = []
    for i in range(8):
        cp = pltpu.make_async_copy(
            h_ref.at[pl.ds(i * 128, 128)], XN.at[pl.ds(i * 128, 128)], hs.at[i]
        )
        hcp.append(cp)
    own_w = pltpu.make_async_copy(
        w_ref.at[:, pl.ds(mo(c * 512, 512), 512)], WO.at[c], ls.at[0]
    )
    slab_cp = pltpu.make_async_copy(slab_ref, SLAB, ls.at[1])
    own_w.start()
    hcp[0].start()

    peers = []
    for dx in range(4):
        for fl in range(2):
            for dc in range(2):
                if (dx, fl, dc) != (0, 0, 0):
                    peers.append(dev(xs(dx), y, zf if fl else z, oc if dc else c))
    for d in (1, 2, 3):
        peers.append(dev(x, ys(d), z, c))
    zg = zh * 2 + (1 - zl)
    zo = 3 - zg
    for zz in (zg, zo):
        peers.append(dev(x, y, zz, c))
    for d in (1, 2, 3):
        peers.append(dev(x, ys(d), zg, c))
    bar = pltpu.get_barrier_semaphore()
    for p in peers:
        pl.semaphore_signal(bar, inc=1, device_id=p, device_id_type=MESH)
    pl.semaphore_wait(bar, len(peers))

    started = []

    def send(src, dst, to):
        k = len(started)
        cp = pltpu.make_async_remote_copy(
            src_ref=src, dst_ref=dst, send_sem=ss.at[k], recv_sem=rs.at[k],
            device_id=to, device_id_type=MESH,
        )
        cp.start()
        started.append(cp)
        return cp

    def recv(cps):
        for cp in cps:
            cp.wait_recv()

    sib = dev(x, y, z, oc)
    k_w = send(w_ref.at[:, pl.ds(mo(oc * 512, 512), 512)], WO.at[c], sib)
    for i in range(1, 8):
        hcp[i].start()
    slab_cp.start()
    TN[...] = jnp.zeros_like(TN)
    TN[0:32, 0:64] = neg_ref[...]
    NG[y] = jnp.transpose(TN[...])[0:64, :]
    k_neg = [
        send(NG.at[y], NG.at[y], dev(x, ys(d), z, c)) for d in (1, 2, 3)
    ]
    GN[...] = gain_ref[...].astype(F32).reshape(1, 4096)

    wf = jnp.sum(w_ref[...].astype(F32) * pq, axis=1, keepdims=True)
    vcol = mo(f_i * 256, 256)
    V[:, pl.ds(vcol, 256)] = col_to_row(wf, 256)
    k_v = []
    for dx in range(4):
        for fl in range(2):
            for dc in range(2):
                if (dx, fl, dc) != (0, 0, 0):
                    k_v.append(
                        send(
                            V.at[:, pl.ds(vcol, 256)], V.at[:, pl.ds(vcol, 256)],
                            dev(xs(dx), y, zf if fl else z, oc if dc else c),
                        )
                    )

    own_w.wait()
    k_w.wait_recv()
    cx = pl.ds(*COLX)
    cy = pl.ds(*COLY)
    cz = pl.ds(*COLZ)
    wo5 = WO.reshape(2, 2, 4, 32, 512)
    def xnb(d):
        return dev(xs(d), y, z, c)

    def ynb(d):
        return dev(x, ys(d), z, c)

    def znb(d):
        return dev(x, y, zs(d), c)

    k_xp = send(wo5.at[:, :, :, :, cx], WH.at[x, zh, :, :, :, :, cx], dev(x, y, zf, c))
    k_yp = {}
    for dx, fl in ((0, 1), (1, 0), (3, 0), (1, 1), (3, 1), (2, 0), (2, 1)):
        k_yp[dx, fl] = send(
            wo5.at[:, :, y, :, cy], WH.at[x, zh, :, :, y, :, cy],
            dev(xs(dx), y, zf if fl else z, c),
        )
    k_zp = [
        send(wo5.at[:, zl, :, :, cz], WH.at[x, zh, :, zl, :, :, cz], xnb(d))
        for d in (1, 3, 2)
    ]
    k_xm = [
        send(wo5.at[:, :, :, :, cx], WH.at[x, zh, :, :, :, :, cx], xnb(d))
        for d in (1, 3)
    ]
    for ci in range(2):
        for a in range(2):
            WH[x, zh, ci, a, :, :, 0:384] = wo5[ci, a, :, :, 0:384]
        WH[x, zh, ci, zl, :, :, cz] = wo5[ci, zl, :, :, cz]

    near = []
    far = []

    def step_x2():
        k_xp.wait_recv()
        r = WH.at[x, 1 - zh, :, :, :, :, cx]
        return [send(r, r, xnb(d)) for d in (1, 3)]

    def step_y(dx):
        for fl in range(2):
            if (dx, fl) != (0, 0):
                k_yp[dx, fl].wait_recv()
        xg = xs(4 - dx)
        r = WH.at[x, 1 - zh, :, :, y, :, cy] if dx == 0 else WH.at[xg, :, :, :, y, :, cy]
        return [send(r, r, ynb(d)) for d in (1, 3)]

    def step_z():
        recv(k_zp)
        r = WH.at[:, zh, :, zl, :, :, cz]
        return [send(r, r, znb(d)) for d in (1, 3)]

    def relay(cps, reg, nb, rest):
        cps[0].wait_recv()
        r = reg(3, 0)
        rest.append(send(r, r, nb(1)))
        cps[1].wait_recv()
        r = reg(1, 1)
        rest.append(send(r, r, nb(3)))

    def relay_x(cps, zz):
        relay(cps, lambda d, h: WH.at[xs(d), zz, h, :, :, :, cx], xnb, far)

    def relay_y(cps, dx):
        if dx == 0:
            relay(cps, lambda d, h: WH.at[x, 1 - zh, h, :, ys(d), :, cy], ynb, near)
        else:
            relay(cps, lambda d, h: WH.at[xs(4 - dx), :, h, :, ys(d), :, cy], ynb, far if dx == 2 else near)

    def relay_z(cps):
        def reg(d, h):
            zz = zs(d)
            return WH.at[:, zz // 2, h, lax.rem(zz, 2), :, :, cz]

        relay(cps, reg, znb, near)

    def norm_rows(i, carry):
        r = pl.ds(mo(i * 16, 16), 16)
        ms = jnp.zeros((16, 128), F32)
        for j in range(8):
            xv = XN[r, j * 512 : (j + 1) * 512].astype(F32)
            sq = xv * xv
            ms = ms + ((sq[:, 0:128] + sq[:, 128:256]) + (sq[:, 256:384] + sq[:, 384:512]))
        inv = lax.rsqrt(jnp.sum(ms, axis=1, keepdims=True) / 4096.0 + NORM_EPS)
        for j in range(8):
            cs = slice(j * 512, (j + 1) * 512)
            XN[r, cs] = (
                XN[r, cs].astype(F32) * inv * GN[:, cs]
            ).astype(BF)
        return carry

    def norm_chunk(i):
        hcp[i].wait()
        lax.fori_loop(i * 8, i * 8 + 8, norm_rows, 0, unroll=2)

    norm_chunk(0)
    norm_chunk(1)
    k_y0 = step_y(0)
    k_xm2 = step_x2()
    norm_chunk(2)
    norm_chunk(3)
    k_y1 = step_y(1)
    k_y3 = step_y(3)
    norm_chunk(4)
    norm_chunk(5)
    k_y2 = step_y(2)
    k_zm = step_z()
    norm_chunk(6)
    norm_chunk(7)

    recv(k_v)

    def gate_rows(i, carry):
        r = pl.ds(mo(i * 16, 16), 16)
        acc = jnp.zeros((16, 128), F32)
        for j in range(8):
            cs = slice(j * 512, (j + 1) * 512)
            p = XN[r, cs].astype(F32) * V[:, cs]
            acc = acc + ((p[:, 0:128] + p[:, 128:256]) + (p[:, 256:384] + p[:, 384:512]))
        LG[r, :] = jnp.broadcast_to(jnp.sum(acc, axis=1, keepdims=True), (16, 128))
        n = jnp.full((16, 128), len_ref[i], jnp.int32)
        slot = lax.broadcasted_iota(jnp.int32, (16, 128), 0)
        WT[r, :] = jnp.where(slot < n, 1.0, 0.0) / n.astype(F32)
        return carry

    lax.fori_loop(0, 32, gate_rows, 0, unroll=2)
    relay_y(k_y0, 0)
    lax.fori_loop(32, 64, gate_rows, 0, unroll=2)
    relay_y(k_y1, 1)
    relay_x(k_xm, zh)

    def at_rows(i, carry):
        r = pl.ds(mo(i * 256, 256), 256)
        gate = jax.nn.sigmoid(LG[r, :] * (1.0 / 32.0))
        LG[r, :] = gate
        wg = gate * WT[r, :]
        q = (lax.broadcasted_iota(jnp.int32, (256, 128), 0) + i * 256) // 16
        lane = lax.broadcasted_iota(jnp.int32, (256, 128), 1)
        hi = wg.astype(BF).astype(F32)
        a = jnp.where(lane == q, hi, 0.0) + jnp.where(lane == q + 64, wg - hi, 0.0)
        AT[:, r] = jnp.transpose(a).astype(BF)
        return carry

    lax.fori_loop(0, 4, at_rows, 0)

    qrow = mo(c * 64, 64)

    def n_cols(i, carry):
        cs = pl.ds(mo(i * 512, 512), 512)
        rr = jnp.dot(AT[...], XN[:, cs], preferred_element_type=F32)
        hi, lo = split2(rr[:64] + rr[64:])
        NB[0, pl.ds(qrow, 64), cs] = hi
        NB[1, pl.ds(qrow, 64), cs] = lo
        return carry

    lax.fori_loop(0, 4, n_cols, 0)
    relay_y(k_y3, 3)
    relay_x(k_xm2, 1 - zh)
    lax.fori_loop(4, 8, n_cols, 0)
    relay_z(k_zm)
    relay_y(k_y2, 2)
    k_n = send(NB.at[:, pl.ds(qrow, 64), :], NB.at[:, pl.ds(qrow, 64), :], sib)

    slab_cp.wait()
    for i in range(4):
        sv = SLAB[i * 256 : (i + 1) * 256, :].astype(F32)
        sm = lax.rsqrt(jnp.sum(sv * sv, axis=1, keepdims=True) / 1024.0 + EMB_EPS)
        SCR[:, i * 256 : (i + 1) * 256] = col_to_row(sm * (1.0 / (32.0 * TEMP)), 256)
    recv(k_neg)

    def count_rows(i, carry):
        src = i // 4
        r = pl.ds(mo(lax.rem(i, 4) * 16, 16), 16)
        ids = NG[src, r, :] - y * 1024
        row = lax.broadcasted_iota(jnp.int32, (16, 128), 1)
        cnt = [jnp.zeros((16, 128), F32) for _ in range(8)]
        for k in range(8):
            own = [
                jnp.broadcast_to(ids[:, 8 * o + k : 8 * o + k + 1], (16, 128))
                for o in range(4)
            ]
            idb = jnp.where(y < 2, jnp.where(y == 0, own[0], own[1]), jnp.where(y == 2, own[2], own[3]))
            idb = idb - row
            for t in range(8):
                cnt[t] = cnt[t] + jnp.where(idb == t * 128, 1.0, 0.0)
        for t in range(8):
            CM[pl.ds(mo(i * 16, 16), 16), t * 128 : (t + 1) * 128] = cnt[t]
        return carry

    lax.fori_loop(0, 16, count_rows, 0)

    k_n.wait_recv()

    def nt_block(i, carry):
        xi = i // 2
        zi = lax.rem(i, 2)
        cs = pl.ds(mo(xi * 1024 + zi * 512 + c * 256, 256), 256)
        for p in range(2):
            t = jnp.transpose(NB[p, :, cs].astype(F32)).astype(BF)
            NT[xi, 2 * zi, p] = t[0:128]
            NT[xi, 2 * zi + 1, p] = t[128:256]
        return carry

    lax.fori_loop(0, 8, nt_block, 0)

    ACC[...] = jnp.zeros_like(ACC)

    def pool_k(k, carry):
        o = k // 4
        xk = lax.rem(x + o + o // 2 - 2 * (o // 3), 4)
        w = WH[xk, lax.rem(k // 2, 2), lax.rem(k, 2)].reshape(256, 512)
        a = NB[:, :, pl.ds(mo(xk * 1024 + lax.rem(k, 4) * 256, 256), 256)].reshape(256, 256)
        ACC[...] += jnp.dot(a, w, preferred_element_type=F32)
        return carry

    recv(near)
    k_nt = [send(NT.at[xs(d)], NTX.at[d - 1], xnb(d)) for d in (1, 2, 3)]
    k_nt += [send(NT.at[:, zs(d)], NTZ.at[d - 1], znb(d)) for d in (1, 2, 3)]


    lax.fori_loop(0, 12, pool_k, 0)
    recv(far)
    lax.fori_loop(12, 16, pool_k, 0)
    orow = mo(oc * 64, 64)
    PO[c] = ACC[pl.ds(qrow, 64), :] + ACC[pl.ds(128 + qrow, 64), :]
    PO[2 + c] = ACC[pl.ds(orow, 64), :] + ACC[pl.ds(128 + orow, 64), :]
    k_po = send(PO.at[2 + c], PO.at[c], sib)
    k_po.wait_recv()
    pooled = jnp.concatenate([PO[0], PO[1]], axis=1)
    mean_sq = jnp.mean(pooled * pooled, axis=1, keepdims=True)
    unit = lax.rsqrt(mean_sq + EMB_EPS) / 32.0
    emb = (pooled * unit).astype(BF)
    EA[y] = emb
    k_e = {d: send(EA.at[y], EA.at[y], ynb(d)) for d in (1, 3, 2)}

    posf = pos_ref[...].astype(F32)
    pm = lax.rsqrt(jnp.mean(posf * posf, axis=1, keepdims=True) + EMB_EPS) * (
        1.0 / (32.0 * TEMP)
    )
    ps = jnp.sum(emb.astype(F32) * posf, axis=1, keepdims=True) * pm
    pe = jnp.exp(ps)

    def score(g):
        y0, y1 = (ys(3), ys(1)) if g == 0 else (ys(2), y)
        ea = jnp.concatenate([EA[y0], EA[y1]], axis=0)
        den = jnp.zeros((128, 1), F32)
        for i in range(4):
            cs = slice(i * 256, (i + 1) * 256)
            s = lax.dot_general(
                ea, SLAB[cs, :], (((1,), (1,)), ((), ())), preferred_element_type=F32
            )
            cnt = jnp.concatenate(
                [CM[pl.ds(mo(y0 * 64, 64), 64), cs], CM[pl.ds(mo(y1 * 64, 64), 64), cs]], axis=0
            )
            ew = jnp.exp(s * SCR[:, cs]) * cnt
            den = den + jnp.sum(ew, axis=1, keepdims=True)
            WB[:, cs] = (ew * SCR[:, cs]).astype(BF)
        den = jnp.broadcast_to(den, (128, 128))
        DS[y0] = den[0:64]
        DS[y1] = den[64:128]
        for i in range(2):
            cs = slice(i * 512, (i + 1) * 512)
            gr = jnp.dot(WB[...], SLAB[:, cs], preferred_element_type=F32).astype(BF)
            GS[y0, :, cs] = gr[0:64]
            GS[y1, :, cs] = gr[64:128]

    k_e[1].wait_recv()
    k_e[3].wait_recv()
    score(0)
    k_g = [send(GS.at[ys(d)], GR.at[d - 1], ynb(d)) for d in (1, 3)]
    k_d = [send(DS.at[ys(d)], DR.at[d - 1], ynb(d)) for d in (1, 3)]
    k_e[2].wait_recv()
    score(1)
    k_g.append(send(GS.at[ys(2)], GR.at[1], ynb(2)))
    k_d.append(send(DS.at[ys(2)], DR.at[1], ynb(2)))
    recv(k_d)
    denom = pe + (DS[y] + DR[0] + DR[1] + DR[2])[:, 0:1]
    rden = 1.0 / denom
    loss = jnp.sum(jnp.log(denom) - ps, axis=0, keepdims=True)
    Z[0, :, 4096:4224] = jnp.broadcast_to(loss, (1, 128))
    recv(k_g)
    gsum = (
        GS[y].astype(F32) + GR[0].astype(F32) + GR[1].astype(F32) + GR[2].astype(F32)
    )
    g_emb = (pe * rden - 1.0) * pm * posf + gsum * rden
    radial = jnp.sum(pooled * g_emb, axis=1, keepdims=True)
    g_pool = unit * g_emb - pooled * (radial * unit / (1024.0 * (mean_sq + EMB_EPS)))
    hi, lo = split2(g_pool)
    GP[0, pl.ds(qrow, 64), :] = hi
    GP[1, pl.ds(qrow, 64), :] = lo
    k_gp = send(GP.at[:, pl.ds(qrow, 64), :], GP.at[:, pl.ds(qrow, 64), :], sib)
    k_gp.wait_recv()

    k_gx = [send(GP.at[0, :, 0:512], GAX.at[d - 1], xnb(d)) for d in (1, 3, 2)]
    k_gz = [send(GP.at[0, :, 512:1024], GAZ.at[d - 1], znb(d)) for d in (1, 3, 2)]

    gph = GP[:, :, pl.ds(mo(c * 512, 512), 512)].reshape(256, 512)

    def u_block(k, carry):
        w = WH[k // 4, lax.rem(k // 2, 2), lax.rem(k, 2)].reshape(256, 512)
        u = lax.dot_general(gph, w, (((1,), (1,)), ((), ())), preferred_element_type=F32)
        UP[:, pl.ds(mo(k * 256, 256), 256)] = u[:128] + u[128:]
        return carry

    lax.fori_loop(0, 16, u_block, 0)
    k_u = send(UP.at[pl.ds(orow, 64), :], UR, sib)

    recv(k_nt)

    def fac_pair(n0, n1, g0, g1):
        out = None
        gg = jnp.concatenate([g0, g1], axis=0)
        for p in range(2):
            nn = jnp.concatenate([n0(p).reshape(512, 128), n1(p).reshape(512, 128)], axis=1)
            r = jnp.dot(nn, gg, preferred_element_type=F32)
            out = r if out is None else out + r
        return out

    recv(k_gx)
    PT[...] = fac_pair(lambda p: NT[x, :, p], lambda p: NTX[0, :, p], GP[0, :, 0:512], GAX[0])
    PT[...] += fac_pair(lambda p: NTX[1, :, p], lambda p: NTX[2, :, p], GAX[1], GAX[2])
    PBS[0] = PT[...].astype(BF).reshape(4, 128, 512)
    PA[:, 0:512] = PT[pl.ds(mo(z * 128, 128), 128), :]
    k_pb = [send(PBS.at[0, zs(d)], PBR.at[0, d - 1], znb(d)) for d in (1, 3, 2)]
    recv(k_gz)
    PT[...] = fac_pair(lambda p: NT[:, z, p], lambda p: NTZ[0, :, p], GP[0, :, 512:1024], GAZ[0])
    PT[...] += fac_pair(lambda p: NTZ[1, :, p], lambda p: NTZ[2, :, p], GAZ[1], GAZ[2])
    PBS[1] = PT[...].astype(BF).reshape(4, 128, 512)
    PA[:, 512:1024] = PT[pl.ds(mo(x * 128, 128), 128), :]
    k_pb += [send(PBS.at[1, xs(d)], PBR.at[1, d - 1], xnb(d)) for d in (1, 3, 2)]

    k_u.wait_recv()
    SACC[...] = jnp.zeros_like(SACC)

    def slope_rows(i, carry):
        r = pl.ds(mo(i * 16, 16), 16)
        uo = pl.ds(qrow + i, 1)
        acc = jnp.zeros((16, 128), F32)
        for j in range(8):
            cs = slice(j * 512, (j + 1) * 512)
            u = UP[uo, cs] + UR[pl.ds(i, 1), cs]
            p = XN[r, cs].astype(F32) * u
            acc = acc + ((p[:, 0:128] + p[:, 128:256]) + (p[:, 256:384] + p[:, 384:512]))
        pd = jnp.sum(acc, axis=1, keepdims=True)
        gate = LG[r, 0:1]
        slope = WT[r, 0:1] * gate * (1.0 - gate) * pd
        for j in range(8):
            cs = slice(j * 512, (j + 1) * 512)
            SACC[:, cs] += XN[r, cs].astype(F32) * slope
        return carry

    lax.fori_loop(0, 64, slope_rows, 0, unroll=2)
    Z[0, :, 4224:5248] = jnp.zeros((1, 1024), F32)
    Z[0, :, 0:4096] = jnp.sum(SACC[...], axis=0, keepdims=True)
    ZR[0, c] = Z[0]
    k_z0 = send(Z.at[0], ZR.at[0, c], sib)

    recv(k_pb)
    for k in range(2):
        cs = slice(k * 512, (k + 1) * 512)
        PA[:, cs] += (
            PBR[k, 0].astype(F32) + PBR[k, 1].astype(F32) + PBR[k, 2].astype(F32)
        )
    PCS[...] = PA[...].astype(BF).reshape(4, 32, 1024)
    k_pc = [send(PCS.at[ys(d)], PCR.at[d - 1], ynb(d)) for d in (1, 3, 2)]

    k_z0.wait_recv()
    Z[1] = ZR[0, 0] + ZR[0, 1]
    ZR[1, x] = Z[1]
    k_z1 = [send(Z.at[1, :, 0:4224], ZR.at[1, x, :, 0:4224], xnb(d)) for d in (1, 3, 2)]
    recv(k_z1)
    sx = slice(0, 4224)
    Z[2, :, sx] = (ZR[1, 0, :, sx] + ZR[1, 1, :, sx]) + (ZR[1, 2, :, sx] + ZR[1, 3, :, sx])

    row16 = lax.broadcasted_iota(jnp.int32, (16, 256), 0)
    ACC[0:16, :] = jnp.zeros((16, 512), F32)

    def gq_k(k, carry):
        w = WH[k // 4, lax.rem(k // 2, 2), lax.rem(k, 2)].reshape(256, 512)
        sv = Z[2, :, pl.ds(mo(k * 256, 256), 256)]
        h1 = sv.astype(BF).astype(F32)
        r1 = sv - h1
        h2 = r1.astype(BF).astype(F32)
        a = jnp.where(row16 == 0, h1, jnp.where(row16 == 1, h2, jnp.where(row16 == 2, r1 - h2, 0.0)))
        ACC[0:16, :] += jnp.dot(a.astype(BF), w, preferred_element_type=F32)
        return carry

    lax.fori_loop(0, 16, gq_k, 0)
    GQ[c] = jnp.sum(ACC[0:16, :], axis=0, keepdims=True)
    k_gq = send(GQ.at[c], GQ.at[c], sib)

    recv(k_pc)
    piece = PA[pl.ds(mo(y * 32, 32), 32), :] + (
        PCR[0].astype(F32) + PCR[1].astype(F32) + PCR[2].astype(F32)
    )
    PG[...] = piece.astype(BF)
    OG[zl, y] = PG[...]
    k_og = [send(PG, OG.at[zl, y], dev(x, ys(d), zg, c)) for d in (2, 1, 3, 0)]
    k_og += [send(PG, OG.at[zl, y], ynb(d)) for d in (2, 1, 3)]

    k_gq.wait_recv()
    Z[2, :, 4224:4736] = GQ[0]
    Z[2, :, 4736:5248] = GQ[1]
    ZR[2, y] = Z[2]
    k_z2 = [send(Z.at[2], ZR.at[2, y], ynb(d)) for d in (1, 3, 2)]
    recv(k_z2)
    Z[3] = (ZR[2, 0] + ZR[2, 1]) + (ZR[2, 2] + ZR[2, 3])
    ZR[3, z] = Z[3]
    k_z3 = [send(Z.at[3], ZR.at[3, z], znb(d)) for d in (1, 3, 2)]
    recv(k_z3)
    Z[4] = (ZR[3, 0] + ZR[3, 1]) + (ZR[3, 2] + ZR[3, 3])
    sblk_ref[...] = Z[4, :, pl.ds(vcol, 256)]
    zt_ref[...] = Z[4, :, 4096:5248]
    recv(k_og)
    out_ref[...] = OG[...].reshape(256, 1024)

    for cp in started:
        cp.wait_send()


def finish(og_ref, s_ref, z_ref, pq_ref, out_ref, gq_ref, loss_ref):
    col = jnp.transpose(jnp.broadcast_to(s_ref[...] * (1.0 / 32.0), (128, 256)))[:, 0:1]
    out_ref[...] = og_ref[...].astype(F32) + col * pq_ref[...].reshape(1, 1024)
    gq_ref[...] = (z_ref[:, 128:1152] * (1.0 / 32.0)).reshape(1024)
    loss_ref[...] = z_ref[:, 0:128] * (1.0 / 8192.0)


def body(hidden_states, positives, negatives, lengths, norm_gain, proj_weight, pool_query, slab):
    vm = pl.BlockSpec(memory_space=pltpu.VMEM)
    anyspace = pl.BlockSpec(memory_space=pl.ANY)
    scratch = [
        pltpu.VMEM((1024, 4096), BF),
        pltpu.VMEM((2, 256, 512), BF),
        pltpu.VMEM((4, 2, 2, 2, 4, 32, 512), BF),
        pltpu.VMEM((1, 4096), F32),
        pltpu.VMEM((1024, 1024), BF),
        pltpu.VMEM((1, 1024), F32),
        pltpu.VMEM((128, 128), jnp.int32),
        pltpu.VMEM((4, 64, 128), jnp.int32),
        pltpu.VMEM((256, 1024), F32),
        pltpu.VMEM((1024, 128), F32),
        pltpu.VMEM((1024, 128), F32),
        pltpu.VMEM((1, 4096), F32),
        pltpu.VMEM((128, 1024), BF),
        pltpu.VMEM((2, 128, 4096), BF),
        pltpu.VMEM((256, 512), F32),
        pltpu.VMEM((4, 64, 512), F32),
        pltpu.VMEM((4, 64, 1024), BF),
        pltpu.VMEM((128, 1024), BF),
        pltpu.VMEM((4, 64, 1024), BF),
        pltpu.VMEM((3, 64, 1024), BF),
        pltpu.VMEM((4, 64, 128), F32),
        pltpu.VMEM((3, 64, 128), F32),
        pltpu.VMEM((2, 128, 1024), BF),
        pltpu.VMEM((4, 4, 2, 128, 128), BF),
        pltpu.VMEM((3, 4, 2, 128, 128), BF),
        pltpu.VMEM((3, 4, 2, 128, 128), BF),
        pltpu.VMEM((3, 128, 512), BF),
        pltpu.VMEM((3, 128, 512), BF),
        pltpu.VMEM((512, 512), F32),
        pltpu.VMEM((128, 1024), F32),
        pltpu.VMEM((2, 4, 128, 512), BF),
        pltpu.VMEM((2, 3, 128, 512), BF),
        pltpu.VMEM((4, 32, 1024), BF),
        pltpu.VMEM((3, 32, 1024), BF),
        pltpu.VMEM((32, 1024), BF),
        pltpu.VMEM((2, 4, 32, 1024), BF),
        pltpu.VMEM((128, 4096), F32),
        pltpu.VMEM((64, 4096), F32),
        pltpu.VMEM((16, 4096), F32),
        pltpu.VMEM((5, 1, 5248), F32),
        pltpu.VMEM((4, 4, 1, 5248), F32),
        pltpu.VMEM((2, 1, 512), F32),
        pltpu.SemaphoreType.DMA((N_SEM,)),
        pltpu.SemaphoreType.DMA((N_SEM,)),
        pltpu.SemaphoreType.DMA((8,)),
        pltpu.SemaphoreType.DMA((2,)),
    ]
    og, sblk, zt = pl.pallas_call(
        kernel,
        out_shape=(
            jax.ShapeDtypeStruct((256, 1024), BF),
            jax.ShapeDtypeStruct((1, 256), F32),
            jax.ShapeDtypeStruct((1, 1152), F32),
        ),
        in_specs=[anyspace, vm, vm, pl.BlockSpec(memory_space=pltpu.SMEM), vm, vm, vm, anyspace],
        out_specs=(vm, vm, vm),
        scratch_shapes=scratch,
        compiler_params=pltpu.CompilerParams(
            collective_id=0, has_side_effects=True, vmem_limit_bytes=60 * 2**20
        ),
    )(
        hidden_states.reshape(1024, 4096), positives, jnp.transpose(negatives), lengths,
        norm_gain, proj_weight, pool_query, slab,
    )
    grad, gq, loss = pl.pallas_call(
        finish,
        out_shape=(
            jax.ShapeDtypeStruct((256, 1024), F32),
            jax.ShapeDtypeStruct((1024,), F32),
            jax.ShapeDtypeStruct((1, 128), F32),
        ),
        in_specs=[vm, vm, vm, vm],
        out_specs=(vm, vm, vm),
    )(og, sblk, zt, pool_query)
    return grad, gq, loss[0, 0]


def solution(mesh):
    return jax.shard_map(
        body,
        mesh=mesh,
        in_specs=(
            P(("grp", "fsdp", "item"), None, None),
            P(("grp", "fsdp", "item"), None),
            P(("grp", "fsdp", "item"), None),
            P(("grp", "fsdp", "item")),
            P(),
            P("fsdp", None),
            P(),
            P("item", None),
        ),
        out_specs=(P("fsdp", None), P(), P()),
        check_vma=False,
    )
```

time: 138 us -> 107 us (0.78)
  Pallas kernels: 125 us -> 106 us
  local copies, waits for them, and re-layouts: 7.44 us -> 0 us
  between operations: 2.42 us -> 0.64 us
  other arithmetic: 1.4 us -> 0 us
    pallas_call x1 -> x2, Pallas kernels: 125 us -> 106 us  [the longest x1 104 us: body(): pl.pallas_call(kernel, out_shape=(jax.ShapeDtypeStruct((256, 1024), BF),...]
    unnamed x2 -> x0, local copies, waits for them, and re-layouts: 3.57 us -> none
    reshape x2 -> x0, local copies, waits for them, and re-layouts: 2.11 us -> none  [the longest x1 1.3 us: body(): norm_gain.reshape(1, 4096)]
where the time goes in v2:
time: 107 us
  Pallas kernels  106 us (99%)
    pallas_call x1, Pallas kernels, body(): pl.pallas_call(kernel, out_shape=(jax.ShapeDtypeStruct((256, 1024), BF),...  104 us
    pallas_call x1, Pallas kernels, body(): pl.pallas_call(finish, out_shape=(jax.ShapeDtypeStruct((256, 1024), F32),...  2.26 us

profile of v2, /device:TPU:0, one launch (start us, length us, event | category | flops | bytes accessed | tf_op | source)
XLA Modules:
  0.0 106.6 jit_solution(6420763766858432192)
XLA Ops:
  0.6 103.7 %shard_map.103 = (bf16[256,1024]{1,0:T(8,128)(2,1)}, f32[1,256]{1,0:T(1,128)}, f32[1,1152]{1,0:T(1,128)}) custom-call(bf16[1024,4096]{1,0:T(8,128)(2,1)} %bitcast.4, bf16[64,1024]{1,0:T(8,128)(2,1)} %pos_ref.1, s32[32,64]{1,0:T(8,128)} %bitcast.5, s32[64]{0:T(128)} %len_ref.1, bf16[4096]{0:T(1024)(128)(2,1)} %gain_ref.1, bf16[256,1024]{1,0:T(8,128)(2,1)} %w_ref.1, ...), custom_call_target="tpu_custom_call" | custom-call | tf_op jit(solution)/shard_map/pallas_call | solution.py:629
  104.3 2.3 %shard_map.104 = (f32[256,1024]{1,0:T(8,128)}, f32[1024]{0:T(1024)}, f32[1,128]{1,0:T(1,128)}) custom-call(bf16[256,1024]{1,0:T(8,128)(2,1)} %get-tuple-element.9.og_ref, f32[1,256]{1,0:T(1,128)} %get-tuple-element.10.s_ref, f32[1,1152]{1,0:T(1,128)} %get-tuple-element.11.z_ref, f32[1024]{0:T(1024)} %pq_ref.1), custom_call_target="tpu_custom_call" | custom-call | tf_op jit(solution)/shard_map/pallas_call | solution.py:646
